TPU v7x, 128 devices: a whole 4x4x4 slice. The times are simulated.
128 devices in a mesh: freq: 32 (over y_lo, x, z), blk: 4 (over y_hi, core).
Axes of the slice: x: 4, y: 4 (y_hi: 2, y_lo: 2; y = y_hi * 2 + y_lo), z: 4, core: 2. Of those that a mesh axis runs over, the one named last changes fastest.
Arguments:
- voltages: int32 [2, 512, 262144], P(None, 'blk', 'freq'), may hold values from -8 to 7
- taps: int32 [4, 1024], replicated, may hold values from -32 to 127
Outputs:
- visibilities: float32 [2, 1024, 512, 512], P(None, 'freq', 'blk')
All inputs are finite; a program needn't handle non-finite values.
Results may differ from a plain program's by a relative error of at most 0.00065.
Values may be sent and summed in bfloat16 or wider, within the bound.
A program may use at most 128 MiB of HBM per device.

v0:
```python
import math

import jax
import jax.numpy as jnp
from jax import lax
from jax.sharding import PartitionSpec as P


def from_behind(shard, axis, by):
    size = lax.axis_size(axis)
    pairs = [(i, i + by) for i in range(size) if 0 <= i + by < size]
    return lax.ppermute(shard, axis, pairs)


def passed_along(value, axis, steps):
    count = lax.axis_size(axis)
    pairs = [(source, (source + steps) % count) for source in range(count)]
    return lax.ppermute(value, axis, pairs)


def dft_table(channels):
    row_index = lax.broadcasted_iota(jnp.int32, (channels, channels), 0)
    col_index = lax.broadcasted_iota(jnp.int32, (channels, channels), 1)
    phase = (row_index * col_index % channels).astype(jnp.float32) * (2.0 * math.pi / channels)
    factor = 1.0 / math.sqrt(channels)
    cosine = (jnp.cos(phase) * factor).astype(jnp.bfloat16)
    sine = (jnp.sin(phase) * factor).astype(jnp.bfloat16)
    upper = jnp.concatenate([cosine, -sine], axis=1)
    lower = jnp.concatenate([sine, cosine], axis=1)
    return jnp.concatenate([upper, lower], axis=0)


def local(voltages, taps):
    ntaps = taps.shape[0]
    channels = taps.shape[1]
    inputs_blk = voltages.shape[1]
    frames = voltages.shape[2] // channels
    volts = (
        voltages.astype(jnp.float32).reshape(2, inputs_blk, frames, channels).transpose(2, 1, 0, 3)
    )
    coeffs = taps.astype(jnp.float32) / 1024.0
    padded = jnp.pad(volts, ((ntaps - 1, ntaps - 1), (0, 0), (0, 0), (0, 0)))
    span = frames + ntaps - 1
    filtered = jnp.zeros((span, inputs_blk, 2, channels), jnp.float32)
    for tap in range(ntaps):
        filtered = filtered + coeffs[tap][None, None, None, :] * padded[tap : tap + span]
    leftover = filtered[frames:]
    arrived = from_behind(leftover, "freq", 1)
    summed = jnp.concatenate(
        [filtered[: ntaps - 1] + arrived, filtered[ntaps - 1 : frames]], axis=0
    )
    weighted = summed.astype(jnp.bfloat16).reshape(frames * inputs_blk, 2 * channels)
    spectra = jnp.dot(weighted, dft_table(channels), preferred_element_type=jnp.float32)
    spectra = spectra.astype(jnp.bfloat16).reshape(frames, inputs_blk, 2, channels)
    turned = lax.all_to_all(spectra, "freq", split_axis=3, concat_axis=0, tiled=True)
    factor = 1.0 / math.sqrt(turned.shape[0])
    group = turned.shape[3]
    count = lax.axis_size("blk")
    here = lax.axis_index("blk")

    def correlate(tile):
        rotated = jnp.stack([-tile[:, :, 1], tile[:, :, 0]], axis=2)
        partner = jnp.stack([tile, rotated], axis=2)
        return (
            jnp.einsum("sirc,sjorc->ocij", turned, partner, preferred_element_type=jnp.float32)
            * factor
        )

    def place(visible, block, source):
        offset = source * inputs_blk
        zero = jnp.zeros((), jnp.int32)
        return lax.dynamic_update_slice(visible, block, (zero, zero, zero, offset))

    visible = jnp.zeros((2, group, inputs_blk, inputs_blk * count), jnp.float32)
    visible = place(visible, correlate(turned), here)

    def advance(step, carry):
        tile, acc = carry
        tile = passed_along(tile, "blk", 1)
        source = (here - step + count) % count
        return (tile, place(acc, correlate(tile), source))

    carried = lax.fori_loop(1, count, advance, (turned, visible))
    visible = carried[1]
    return visible


def solution(mesh):
    in_specs = (P(None, "blk", "freq"), P())
    out_specs = P(None, "freq", "blk", None)
    return jax.shard_map(local, mesh=mesh, in_specs=in_specs, out_specs=out_specs, check_vma=False)
```

profile of v0, /device:TPU:1, one launch (start us, length us, event | category | flops | bytes accessed | tf_op | source)
XLA Modules:
  0.0 471.7 jit_solution(16865643522374621758)
XLA Ops:
  0.7 8.9 %copy.26 = s32[2,128,8192]{1,2,0:T(8,128)} copy(s32[2,128,8192]{2,1,0:T(8,128)} %param.4) | data formatting | bytes 16777216 | tf_op args[0]
  9.6 3.9 convert_element_type.36
  13.5 4.6 fusion.13
  18.1 4.4 copy-done.3
  26.8 6.0 %collective-permute-start.1 = (f32[3,128,2,1024]{3,1,2,0:T(8,128)S(1)}, f32[3,128,2,1024]{3,1,2,0:T(8,128)}, u32[]{:S(2)}, u32[]{:S(2)}) collective-permute-start(f32[3,128,2,1024]{3,1,2,0:T(8,128)S(1)} %copy.27), channel_id=1, source_target_pairs={{0,4},{4,8},{8,12},{12,16},{16,20},{20,24},{24,28},{28,32},{32,36}... | collective-permute-start | bytes 9437192 | tf_op jit(solution)/shard_map/ppermute | solution.py:12
  32.8 4.4 slice.114
  37.3 16.5 %fusion.47 = bf16[1024,1024]{1,0:T(8,128)(2,1)} fusion(), kind=kLoop, calls=%fused_computation.58 | loop fusion | flops 19922944 | bytes 2097152 | tf_op jit(solution)/shard_map/neg | solution.py:28
  53.8 17.9 %multiply_convert_fusion = (bf16[1024,1024]{1,0:T(8,128)(2,1)}, bf16[1024,1024]{1,0:T(8,128)(2,1)}) fusion(), kind=kLoop, calls=%fused_computation.46 | loop fusion | flops 18874368 | bytes 4194304 | tf_op jit(solution)/shard_map/convert_element_type | solution.py:27
  71.7 26.2 %collective-permute-done.1 = f32[3,128,2,1024]{3,1,2,0:T(8,128)} collective-permute-done((f32[3,128,2,1024]{3,1,2,0:T(8,128)S(1)}, f32[3,128,2,1024]{3,1,2,0:T(8,128)}, u32[]{:S(2)}, u32[]{:S(2)}) %collective-permute-start.1) | collective-permute-done | bytes 3145760 | tf_op jit(solution)/shard_map/ppermute | solution.py:12
  106.1 25.4 %fusion.36 = bf16[1024,2048]{1,0:T(8,128)(2,1)} fusion(bf16[1024,1024]{1,0:T(8,128)(2,1)} %get-tuple-element.180, bf16[1024,1024]{1,0:T(8,128)(2,1)S(1)} %copy-done.8, bf16[1024,1024]{1,0:T(8,128)(2,1)S(1)} %copy-done.7, bf16[256,8,8,128]{3,2,1,0:T(8,128)(2,1)S(1)} %bitcast.77), kind=kOutput, calls=%fused_computation.51 | convolution fusion | flops 8625586176 | bytes 14680064 | tf_op jit(solution)/shard_map/dot_general | solution.py:53
  131.5 7.8 %reshape.15 = bf16[8,128,2,1024]{3,2,1,0:T(2,128)(2,1)} reshape(bf16[1024,2048]{1,0:T(8,128)(2,1)} %fusion.36) | data formatting | bytes 8388608 | tf_op jit(solution)/shard_map/reshape | solution.py:54
  139.3 15.7 %copy.30 = bf16[8,128,2,1024]{1,2,0,3:T(2,128)(2,1)} copy(bf16[8,128,2,1024]{3,2,1,0:T(2,128)(2,1)} %reshape.15) | data formatting | bytes 8388608 | tf_op jit(solution)/shard_map/reshape | solution.py:54
  155.0 9.7 %all-to-all-start = ((bf16[8,128,2,1024]{1,2,0,3:T(2,128)(2,1)}), bf16[8,128,2,1024]{1,2,0,3:T(2,128)(2,1)}, u32[]{:S(2)}, u32[]{:S(2)}) async-start(bf16[8,128,2,1024]{1,2,0,3:T(2,128)(2,1)} %copy.30), calls=%async_computation | async-start | bytes 8388608 | tf_op jit(solution)/shard_map/all_to_all | solution.py:55
  164.7 53.7 %all-to-all-done = bf16[8,128,2,1024]{1,2,0,3:T(2,128)(2,1)} async-done(((bf16[8,128,2,1024]{1,2,0,3:T(2,128)(2,1)}), bf16[8,128,2,1024]{1,2,0,3:T(2,128)(2,1)}, u32[]{:S(2)}, u32[]{:S(2)}) %all-to-all-start) | async-done | bytes 4194336 | tf_op jit(solution)/shard_map/all_to_all | solution.py:55
  228.2 6.4 %copy.35 = bf16[256,128,2,32]{0,1,2,3:T(8,128)(2,1)} copy(bf16[256,128,2,32]{1,0,2,3:T(8,128)(2,1)} %bitcast.71) | data formatting | bytes 8388608 | tf_op jit(solution)/shard_map/while | solution.py:83
  234.6 3.9 maximum_bitcast_fusion.1
  238.6 8.1 %broadcast_in_dim.3 = f32[2,32,128,512]{2,3,0,1:T(8,128)} broadcast(f32[]{:T(128)} %constant.102.clone.1), dimensions={} | broadcast | bytes 16777220 | tf_op jit(solution)/shard_map/broadcast_in_dim | solution.py:74
  246.6 9.2 %bitcast_dynamic-update-slice_fusion.1 = f32[2,32,128,512]{2,3,0,1:T(8,128)} fusion(f32[2,32,128,512]{2,3,0,1:T(8,128)} %broadcast_in_dim.3, s32[]{:T(128)S(6)} %select_n.46, bf16[32,8,128,2,32]{2,4,0,3,1:T(8,128)(2,1)S(1)} %bitcast.76, bf16[256,128,1,2,32]{1,0,3,4,2:T(8,128)(2,1)} %maximum_bitcast_fusion.1, bf16[256,128,1,2,32]{1,0,3,4,2:T(8,128)(2,1)S(1)} %bitcast.73), kind=kOutput, calls=%fused_computation.44 | convolution fusion | flops 1078984704 | bytes 16777220 | tf_op jit(solution)/shard_map/sirc,sjorc->ocij/dot_general | solution.py:65
  255.9 198.4 %while.17 = (s32[]{:T(128)}, bf16[256,128,2,32]{0,1,2,3:T(8,128)(2,1)}, f32[2,32,128,512]{2,3,0,1:T(8,128)}, bf16[256,128,2,32]{1,0,2,3:T(8,128)(2,1)}, s32[]{:T...) while((s32[]{:T(128)}, ...), condition=%wide.region_1.2_spmd, body=%wide.region_0.1_spmd.sunk | while | flops 1082130432 | bytes 75497824 | solution.py:83
  255.9 5.7 %collective-permute-start = (bf16[256,128,2,32]{0,1,2,3:T(8,128)(2,1)}, bf16[256,128,2,32]{0,1,2,3:T(8,128)(2,1)}, u32[]{:S(2)}, u32[]{:S(2)}) collective-permute-start(bf16[256,128,2,32]{0,1,2,3:T(8,128)(2,1)} %get-tuple-element.228), channel_id=1, source_target_pairs={{0,1},{1,2},{2,3},{3,0},{4,5},{5,6},{6,7},{7,4},{8,9},{9,10},{10,1... | collective-permute-start | bytes 12582920 | tf_op jit(solution)/shard_map/while/body/eval_jaxpr/ppermute | solution.py:18
  261.5 45.8 %collective-permute-done = bf16[256,128,2,32]{0,1,2,3:T(8,128)(2,1)} collective-permute-done((bf16[256,128,2,32]{0,1,2,3:T(8,128)(2,1)}, bf16[256,128,2,32]{0,1,2,3:T(8,128)(2,1)}, u32[]{:S(2)}, u32[]{:S(2)}) %collective-permute-start) | collective-permute-done | bytes 4194336 | tf_op jit(solution)/shard_map/while/body/eval_jaxpr/ppermute | solution.py:18
  312.0 6.5 %bitcast_dynamic-update-slice_fusion.3 = f32[2,32,128,512]{2,3,0,1:T(8,128)} fusion(f32[2,32,128,512]{2,3,0,1:T(8,128)} %get-tuple-element.229, s32[]{:T(128)S(6)} %select_n.61, bf16[256,128,2,32]{1,0,2,3:T(8,128)(2,1)S(1)} %copy-done.2, bf16[256,128,1,2,32]{0,1,3,2,4:T(8,128)(2,1)S(1)} %maximum_bitcast_fusion.3, ...), kind=kOutput, calls=%fused_computation.6.clone.1 | convolution fusion | flops 1078984704 | bytes 16777220 | tf_op jit(solution)/shard_map/while/body/eval_jaxpr/sirc,sjorc->ocij/dot_general | solution.py:65
  318.5 4.6 copy.72
  323.1 4.0 collective-permute-start
  327.1 45.8 %collective-permute-done = bf16[256,128,2,32]{0,1,2,3:T(8,128)(2,1)} collective-permute-done((bf16[256,128,2,32]{0,1,2,3:T(8,128)(2,1)}, bf16[256,128,2,32]{0,1,2,3:T(8,128)(2,1)}, u32[]{:S(2)}, u32[]{:S(2)}) %collective-permute-start) | collective-permute-done | bytes 4194336 | tf_op jit(solution)/shard_map/while/body/eval_jaxpr/ppermute | solution.py:18
  377.5 6.5 %bitcast_dynamic-update-slice_fusion.3 = f32[2,32,128,512]{2,3,0,1:T(8,128)} fusion(f32[2,32,128,512]{2,3,0,1:T(8,128)} %get-tuple-element.229, s32[]{:T(128)S(6)} %select_n.61, bf16[256,128,2,32]{1,0,2,3:T(8,128)(2,1)S(1)} %copy-done.2, bf16[256,128,1,2,32]{0,1,3,2,4:T(8,128)(2,1)S(1)} %maximum_bitcast_fusion.3, ...), kind=kOutput, calls=%fused_computation.6.clone.1 | convolution fusion | flops 1078984704 | bytes 16777220 | tf_op jit(solution)/shard_map/while/body/eval_jaxpr/sirc,sjorc->ocij/dot_general | solution.py:65
  384.0 4.6 copy.72
  388.7 4.0 collective-permute-start
  392.7 45.8 %collective-permute-done = bf16[256,128,2,32]{0,1,2,3:T(8,128)(2,1)} collective-permute-done((bf16[256,128,2,32]{0,1,2,3:T(8,128)(2,1)}, bf16[256,128,2,32]{0,1,2,3:T(8,128)(2,1)}, u32[]{:S(2)}, u32[]{:S(2)}) %collective-permute-start) | collective-permute-done | bytes 4194336 | tf_op jit(solution)/shard_map/while/body/eval_jaxpr/ppermute | solution.py:18
  443.1 6.5 %bitcast_dynamic-update-slice_fusion.3 = f32[2,32,128,512]{2,3,0,1:T(8,128)} fusion(f32[2,32,128,512]{2,3,0,1:T(8,128)} %get-tuple-element.229, s32[]{:T(128)S(6)} %select_n.61, bf16[256,128,2,32]{1,0,2,3:T(8,128)(2,1)S(1)} %copy-done.2, bf16[256,128,1,2,32]{0,1,3,2,4:T(8,128)(2,1)S(1)} %maximum_bitcast_fusion.3, ...), kind=kOutput, calls=%fused_computation.6.clone.1 | convolution fusion | flops 1078984704 | bytes 16777220 | tf_op jit(solution)/shard_map/while/body/eval_jaxpr/sirc,sjorc->ocij/dot_general | solution.py:65
  449.6 4.6 copy.72
  454.2 17.4 %copy.36 = f32[2,32,128,512]{3,2,1,0:T(8,128)} copy(f32[2,32,128,512]{2,3,0,1:T(8,128)} %get-tuple-element.138) | data formatting | bytes 33554432 | tf_op jit(solution)/shard_map/while | solution.py:83
  (38 shorter events, 36.8 us)
Async XLA Ops:
  18.1 4.4 copy-start.3
  26.8 71.1 %collective-permute-start.1 = (f32[3,128,2,1024]{3,1,2,0:T(8,128)S(1)}, f32[3,128,2,1024]{3,1,2,0:T(8,128)}, u32[]{:S(2)}, u32[]{:S(2)}) collective-permute-start(f32[3,128,2,1024]{3,1,2,0:T(8,128)S(1)} %copy.27), channel_id=1, source_target_pairs={{0,4},{4,8},{8,12},{12,16},{16,20},{20,24},{24,28},{28,32},{32,36}... | collective-permute-start | bytes 9437192 | tf_op jit(solution)/shard_map/ppermute | solution.py:12
  100.3 2.7 copy-start.6
  103.4 2.7 copy-start.7
  103.4 2.7 copy-start.8
  155.0 63.4 %all-to-all-start = ((bf16[8,128,2,1024]{1,2,0,3:T(2,128)(2,1)}), bf16[8,128,2,1024]{1,2,0,3:T(2,128)(2,1)}, u32[]{:S(2)}, u32[]{:S(2)}) async-start(bf16[8,128,2,1024]{1,2,0,3:T(2,128)(2,1)} %copy.30), calls=%async_computation | async-start | bytes 8388608 | tf_op jit(solution)/shard_map/all_to_all | solution.py:55
  221.7 2.7 copy-start.4
  224.4 2.0 copy-start
  238.6 8.1 %copy-start.1 = (bf16[32,8,128,2,32]{2,1,0,3,4:T(8,128)(2,1)S(1)}, bf16[32,8,128,2,32]{2,1,0,3,4:T(8,128)(2,1)}, u32[]{:S(2)}) copy-start(bf16[32,8,128,2,32]{2,1,0,3,4:T(8,128)(2,1)} %copy-done) | copy-start | bytes 12582916
  238.6 8.1 %copy-start.5 = (bf16[8,128,2,1024]{1,3,2,0:T(8,128)(2,1)S(1)}, bf16[8,128,2,1024]{1,3,2,0:T(8,128)(2,1)}, u32[]{:S(2)}) copy-start(bf16[8,128,2,1024]{1,3,2,0:T(8,128)(2,1)} %copy-done.4) | copy-start | bytes 12582916
  255.9 51.4 %collective-permute-start = (bf16[256,128,2,32]{0,1,2,3:T(8,128)(2,1)}, bf16[256,128,2,32]{0,1,2,3:T(8,128)(2,1)}, u32[]{:S(2)}, u32[]{:S(2)}) collective-permute-start(bf16[256,128,2,32]{0,1,2,3:T(8,128)(2,1)} %get-tuple-element.228), channel_id=1, source_target_pairs={{0,1},{1,2},{2,3},{3,0},{4,5},{5,6},{6,7},{7,4},{8,9},{9,10},{10,1... | collective-permute-start | bytes 12582920 | tf_op jit(solution)/shard_map/while/body/eval_jaxpr/ppermute | solution.py:18
  309.8 2.2 copy-start.2
  323.1 49.7 %collective-permute-start = (bf16[256,128,2,32]{0,1,2,3:T(8,128)(2,1)}, bf16[256,128,2,32]{0,1,2,3:T(8,128)(2,1)}, u32[]{:S(2)}, u32[]{:S(2)}) collective-permute-start(bf16[256,128,2,32]{0,1,2,3:T(8,128)(2,1)} %get-tuple-element.228), channel_id=1, source_target_pairs={{0,1},{1,2},{2,3},{3,0},{4,5},{5,6},{6,7},{7,4},{8,9},{9,10},{10,1... | collective-permute-start | bytes 12582920 | tf_op jit(solution)/shard_map/while/body/eval_jaxpr/ppermute | solution.py:18
  375.4 2.2 copy-start.2
  388.7 49.7 %collective-permute-start = (bf16[256,128,2,32]{0,1,2,3:T(8,128)(2,1)}, bf16[256,128,2,32]{0,1,2,3:T(8,128)(2,1)}, u32[]{:S(2)}, u32[]{:S(2)}) collective-permute-start(bf16[256,128,2,32]{0,1,2,3:T(8,128)(2,1)} %get-tuple-element.228), channel_id=1, source_target_pairs={{0,1},{1,2},{2,3},{3,0},{4,5},{5,6},{6,7},{7,4},{8,9},{9,10},{10,1... | collective-permute-start | bytes 12582920 | tf_op jit(solution)/shard_map/while/body/eval_jaxpr/ppermute | solution.py:18
  440.9 2.2 copy-start.2
where the time goes:
time: 474 us; the launch traced here: 472 us
  waiting for transfers between devices  217 us (46%)
  local copies, waits for them, and re-layouts  110 us (23%)
  other arithmetic  60.8 us (13%)
  matrix products  54.1 us (11%)
  starting transfers between devices  29.3 us (6%)
    ppermute x3, waiting for transfers between devices, passed_along(): return lax.ppermute(value, axis, pairs)  137 us
    all_to_all x1, waiting for transfers between devices, local(): lax.all_to_all(spectra, 'freq', split_axis=3, concat_axis=0, tiled=True)  53.7 us
    dot_general x4, matrix products, correlate(): jnp.einsum('sirc,sjorc->ocij', turned, partner, preferred_element_type=jn...  28.7 us
    ppermute x1, waiting for transfers between devices, from_behind(): return lax.ppermute(shard, axis, pairs)  26.2 us
    dot_general x1, matrix products, local(): jnp.dot(weighted, dft_table(channels), preferred_element_type=jnp.float32)  25.4 us
    while x2, local copies, waits for them, and re-layouts, local(): carried = lax.fori_loop(1, count, advance, (turned, visible))  23.9 us
    reshape x2, local copies, waits for them, and re-layouts, local(): spectra.astype(jnp.bfloat16).reshape(frames, inputs_blk, 2, channels)  23.5 us
    while x9, local copies, waits for them, and re-layouts  19.3 us
  transfers between devices with their start and end apart: 5, of which 5 were waited for; matrix products, arithmetic and copies ran while one was open for 8% of the time, Pallas kernels for 0%

commit v1 on v0

v1 whole, which is shorter than its diff:
```python
import functools
import math

import jax
import jax.numpy as jnp
import ml_dtypes
import numpy as np
from jax import lax
from jax.experimental import pallas as pl
from jax.experimental.pallas import tpu as pltpu
from jax.sharding import PartitionSpec as P

MESH = pl.DeviceIdType.MESH
CHANNELS = 1024
HALF = CHANNELS // 2
INPUTS = 128
FRAMES = 8
GROUP = 32
PITCH = CHANNELS + 8
CHUNK = 256
LAG = 8


def fourier_rows():
    n = np.arange(CHANNELS)
    k = np.arange(HALF)
    step = np.float32(2.0 * math.pi / CHANNELS)
    scale = np.float32(1.0 / math.sqrt(CHANNELS))
    phase = (np.outer(k, n) % CHANNELS).astype(np.float32) * step
    cosine = np.cos(phase) * scale
    sine = np.sin(phase) * scale
    sine[0] = np.cos((HALF * n % CHANNELS).astype(np.float32) * step) * scale
    both = np.stack([cosine.reshape(-1, CHUNK, CHANNELS), sine.reshape(-1, CHUNK, CHANNELS)], axis=1)
    return both.reshape(CHANNELS, CHANNELS).astype(ml_dtypes.bfloat16)


def position():
    f = lax.axis_index("freq")
    b = lax.axis_index("blk")
    return (f // 4) % 4, (b // 2) * 2 + f // 16, f % 4, b % 2


def device(x, y, z, c):
    return ((y % 2) * 16 + x * 4 + z, (y // 2) * 2 + c)


def offset(i):
    return i % 4, (i // 4 + i) % 4


def turn_kernel(
    volts, taps, table_hbm, out,
    frames, halo_out, halo_in, coeffs, weighted, table, spectra, outbox, inbox,
    load_sem, table_sem, halo_send, halo_recv, plane_send, plane_recv,
    y_send, y_recv, core_send, core_recv, dup_send, dup_recv, keep_sem,
):
    f = lax.axis_index("freq")
    block = lax.axis_index("blk")
    x, y, z, c = position()
    y_lo = y % 2
    here = x * 4 + z
    up = device(x, (y + 1) % 4, z, c)
    down = device(x, (y + 3) % 4, z, c)
    across = device(x, (y + 2) % 4, z, c)
    twin = device(x, y, z, 1 - c)
    after = ((f + 1) % 32, block)
    before = ((f + 31) % 32, block)

    def plane(i, sign):
        dx, dz = offset(i)
        px = (x + 4 + sign * dx) % 4
        pz = (z + 4 + sign * dz) % 4
        return px * 4 + pz, device(px, y, pz, c)

    barrier = pltpu.get_barrier_semaphore()
    for partner in (up, down, across, twin, after, before):
        pl.semaphore_signal(barrier, inc=1, device_id=partner, device_id_type=MESH)

    def greet(i, carry):
        pl.semaphore_signal(barrier, inc=1, device_id=plane(i, 1)[1], device_id_type=MESH)
        return carry

    lax.fori_loop(1, 16, greet, 0)

    def load(s):
        return pltpu.make_async_copy(
            volts.at[:, :, pl.ds(s * CHANNELS, CHANNELS)], frames.at[s], load_sem.at[s]
        )

    table_copy = pltpu.make_async_copy(table_hbm, table, table_sem)
    for s in (5, 6, 7, 4, 3, 2, 1):
        load(s).start()
    table_copy.start()
    load(0).start()

    coeffs[...] = taps[...].astype(jnp.float32) * (1.0 / 1024.0)

    for j in range(3):
        load(5 + j).wait()

        def narrow(t, carry):
            rows = pl.ds(pl.multiple_of(t * 16, 16), 16)
            for r in range(2):
                halo_out[j, r, rows, :] = frames[5 + j, r, rows, :].astype(jnp.bfloat16)
            return carry

        lax.fori_loop(0, INPUTS // 16, narrow, 0)

    pl.semaphore_wait(barrier, 21)
    halo = pltpu.make_async_remote_copy(
        src_ref=halo_out, dst_ref=halo_in, send_sem=halo_send, recv_sem=halo_recv,
        device_id=after, device_id_type=MESH,
    )
    halo.start()

    def filter_half(earlier, first):
        def body(t, carry):
            rows = pl.ds(pl.multiple_of(t * 16, 16), 16)
            for r in range(2):
                for n in range(0, CHANNELS, 256):
                    cols = slice(n, n + 256)
                    seen = [earlier(j, r, rows, cols) for j in range(3)]
                    seen += [frames[first + j, r, rows, cols].astype(jnp.float32) for j in range(4)]
                    scale = [jnp.broadcast_to(coeffs[k : k + 1, cols], (16, 256)) for k in range(4)]
                    for s in range(4):
                        total = scale[0] * seen[s]
                        for k in range(1, 4):
                            total = total + scale[k] * seen[s + k]
                        into = pl.ds(pl.multiple_of(r * INPUTS + t * 16, 16), 16)
                        weighted[s, into, cols] = total.astype(jnp.bfloat16)
            return carry

        lax.fori_loop(0, INPUTS // 16, body, 0)

    def transform_half():
        def body(s, carry):
            rhs = weighted[s]
            re = pl.multiple_of(s * PITCH, 8)
            im = pl.multiple_of((4 + s) * PITCH, 8)
            for q in range(HALF // CHUNK):
                got = lax.dot_general(
                    table[q * 2 * CHUNK : (q + 1) * 2 * CHUNK, :], rhs, (((1,), (1,)), ((), ())),
                    preferred_element_type=jnp.float32,
                )
                a, b = got[:CHUNK, :INPUTS], got[CHUNK:, :INPUTS]
                cc, d = got[:CHUNK, INPUTS:], got[CHUNK:, INPUTS:]
                k = q * CHUNK
                spectra[pl.ds(re + k, CHUNK), :] = a + d
                spectra[pl.ds(im + k, CHUNK), :] = cc - b
                spectra[pl.ds(re + HALF + k, CHUNK), :] = a - d
                spectra[pl.ds(im + HALF + k, CHUNK), :] = cc + b
                if q == 0:
                    spectra[pl.ds(re, 1), :] = a[:1]
                    spectra[pl.ds(im, 1), :] = cc[:1]
                    spectra[pl.ds(re + CHANNELS, 1), :] = b[:1]
                    spectra[pl.ds(im + CHANNELS, 1), :] = d[:1]
            return carry

        lax.fori_loop(0, 4, body, 0)

    def gather(g, into):
        for k in range(GROUP):
            low = spectra[pl.ds(g * GROUP + k, 8, stride=PITCH), :]
            into[0, k] = low.astype(jnp.bfloat16)
            high = spectra[pl.ds(CHANNELS - g * GROUP - k, 8, stride=PITCH), :]
            into[1, k] = high.astype(jnp.bfloat16)

    def plane_copy(h, i):
        g, to = plane(i, 1)
        return pltpu.make_async_remote_copy(
            src_ref=outbox.at[h, g], dst_ref=inbox.at[h, here], send_sem=plane_send.at[h],
            recv_sem=plane_recv.at[h, here], device_id=to, device_id_type=MESH,
        )

    def send_half(h):
        def body(i, carry):
            gather(plane(i, 1)[0], outbox.at[h, plane(i, 1)[0]])
            plane_copy(h, i).start()
            return carry

        lax.fori_loop(1, 16, body, 0)
        gather(here, inbox.at[h, here])

    def forward(h, i):
        j = plane(i, -1)[0]

        @pl.when(i > 0)
        def _():
            pltpu.make_async_remote_copy(
                src_ref=inbox.at[h, j], dst_ref=inbox.at[h, j], send_sem=plane_send.at[h],
                recv_sem=plane_recv.at[h, j], device_id=twin, device_id_type=MESH,
            ).wait_recv()

        theirs = inbox.at[h, j, 1 - y_lo]
        ours = inbox.at[h, j, y_lo]
        slot = out.at[block, h, y_lo * 16 + j]
        for way, (to, chunk) in enumerate(((up, theirs), (down, theirs), (across, ours))):
            pltpu.make_async_remote_copy(
                src_ref=chunk, dst_ref=slot, send_sem=y_send.at[way], recv_sem=y_recv.at[way, h, j],
                device_id=to, device_id_type=MESH,
            ).start()
        pltpu.make_async_remote_copy(
            src_ref=ours, dst_ref=slot, send_sem=core_send, recv_sem=core_recv,
            device_id=twin, device_id_type=MESH,
        ).start()
        pltpu.make_async_copy(ours, slot, keep_sem).start()

    def arrival(way, h, j):
        sender = (y + 3 - 2 * way) % 4 if way < 2 else (y + 2) % 4
        return out.at[(sender // 2) * 2 + c, h, (sender % 2) * 16 + j]

    def duplicate(h, i):
        j = plane(i, -1)[0]
        for way in range(3):
            slot = arrival(way, h, j)
            pltpu.make_async_remote_copy(
                src_ref=slot, dst_ref=slot, send_sem=y_send.at[way], recv_sem=y_recv.at[way, h, j],
                device_id=twin, device_id_type=MESH,
            ).wait_recv()
            pltpu.make_async_remote_copy(
                src_ref=slot, dst_ref=slot, send_sem=dup_send.at[way], recv_sem=dup_recv.at[way],
                device_id=twin, device_id_type=MESH,
            ).start()

    for s in (4, 3, 2, 1):
        load(s).wait()
    filter_half(lambda j, r, rows, cols: frames[1 + j, r, rows, cols].astype(jnp.float32), 4)
    table_copy.wait()
    transform_half()
    send_half(0)

    def first(i, carry):
        forward(0, i)

        @pl.when(i >= LAG)
        def _():
            duplicate(0, i - LAG)

        return carry

    lax.fori_loop(0, 16, first, 0)

    load(0).wait()
    halo.wait()
    live = jnp.where(f > 0, 1.0, 0.0).astype(jnp.float32)
    filter_half(lambda j, r, rows, cols: halo_in[j, r, rows, cols].astype(jnp.float32) * live, 0)
    transform_half()
    send_half(1)

    def second(i, carry):
        forward(1, i)

        @pl.when(i < LAG)
        def _():
            duplicate(0, i + 16 - LAG)

        @pl.when(i >= LAG)
        def _():
            duplicate(1, i - LAG)

        return carry

    lax.fori_loop(0, 16, second, 0)

    def last(i, carry):
        duplicate(1, i)
        return carry

    lax.fori_loop(16 - LAG, 16, last, 0)

    def whole(ref, send_sem, recv_sem):
        return pltpu.make_async_remote_copy(
            src_ref=ref, dst_ref=ref, send_sem=send_sem, recv_sem=recv_sem,
            device_id=twin, device_id_type=MESH,
        )

    for h in range(2):
        whole(outbox.at[h, pl.ds(0, 15)], plane_send.at[h], plane_recv.at[0, 0]).wait_send()
    part = out.at[0, 0]
    for way in range(3):
        whole(part, y_send.at[way], core_recv).wait_send()
        whole(part, dup_send.at[way], core_recv).wait_send()
        whole(part, dup_send.at[way], dup_recv.at[way]).wait_recv()
    whole(part, core_send, core_recv).wait_send()
    whole(part, core_send, core_recv).wait_recv()
    pltpu.make_async_copy(part, part, keep_sem).wait()


def corner_turn(voltages, taps, table):
    bf16 = jnp.bfloat16
    dma = pltpu.SemaphoreType.DMA
    return pl.pallas_call(
        turn_kernel,
        out_shape=jax.ShapeDtypeStruct((4, 2, 32, GROUP, 8, INPUTS), bf16),
        in_specs=[
            pl.BlockSpec(memory_space=pl.ANY),
            pl.BlockSpec(memory_space=pltpu.VMEM),
            pl.BlockSpec(memory_space=pl.ANY),
        ],
        out_specs=pl.BlockSpec(memory_space=pl.ANY),
        scratch_shapes=[
            pltpu.VMEM((FRAMES, 2, INPUTS, CHANNELS), jnp.int32),
            pltpu.VMEM((3, 2, INPUTS, CHANNELS), bf16),
            pltpu.VMEM((3, 2, INPUTS, CHANNELS), bf16),
            pltpu.VMEM((4, CHANNELS), jnp.float32),
            pltpu.VMEM((4, 2 * INPUTS, CHANNELS), bf16),
            pltpu.VMEM((CHANNELS, CHANNELS), bf16),
            pltpu.VMEM((8 * PITCH, INPUTS), jnp.float32),
            pltpu.VMEM((2, 16, 2, GROUP, 8, INPUTS), bf16),
            pltpu.VMEM((2, 16, 2, GROUP, 8, INPUTS), bf16),
            dma((FRAMES,)), dma, dma, dma, dma((2,)), dma((2, 16)),
            dma((3,)), dma((3, 2, 16)), dma, dma, dma((3,)), dma((3,)), dma,
        ],
        compiler_params=pltpu.CompilerParams(
            collective_id=0, has_side_effects=True, vmem_limit_bytes=56 << 20
        ),
        name="corner_turn",
    )(voltages, taps, table)


def correlate_kernel(count, tiles, visible):
    me = lax.axis_index("blk")
    part = lax.broadcasted_iota(jnp.int32, (1, 8, INPUTS), 1)
    sign = jnp.where(part < 4, 0.0625, -0.0625).astype(jnp.float32)
    rows = 64 * 8
    for k in range(count):
        mine = tiles[me, :, k].astype(jnp.float32)
        rotated = pltpu.roll(mine, 4, axis=1) * sign
        left = jnp.concatenate(
            [(mine * 0.0625).reshape(rows, INPUTS), rotated.reshape(rows, INPUTS)], axis=1
        ).astype(jnp.bfloat16)
        for b in range(0, 4, 2):
            right = jnp.concatenate(
                [tiles[b, :, k].reshape(rows, INPUTS), tiles[b + 1, :, k].reshape(rows, INPUTS)], axis=1
            )
            both = lax.dot_general(
                left, right, (((0,), (0,)), ((), ())), preferred_element_type=jnp.float32
            )
            visible[0, k, :, b * INPUTS : (b + 2) * INPUTS] = both[:INPUTS]
            visible[1, k, :, b * INPUTS : (b + 2) * INPUTS] = both[INPUTS:]


def correlate(tiles, count=8):
    return pl.pallas_call(
        functools.partial(correlate_kernel, count),
        grid=(GROUP // count,),
        in_specs=[pl.BlockSpec((4, 64, count, 8, INPUTS), lambda k: (0, 0, k, 0, 0))],
        out_specs=pl.BlockSpec((2, count, INPUTS, 4 * INPUTS), lambda k: (0, k, 0, 0)),
        out_shape=jax.ShapeDtypeStruct((2, GROUP, INPUTS, 4 * INPUTS), jnp.float32),
        compiler_params=pltpu.CompilerParams(vmem_limit_bytes=40 << 20),
        name="correlate",
    )(tiles)


def local(voltages, taps):
    table = jnp.asarray(fourier_rows())
    tiles = corner_turn(voltages, taps, table)
    return correlate(tiles.reshape(4, 64, GROUP, 8, INPUTS))


def solution(mesh):
    in_specs = (P(None, "blk", "freq"), P())
    out_specs = P(None, "freq", "blk", None)
    return jax.shard_map(local, mesh=mesh, in_specs=in_specs, out_specs=out_specs, check_vma=False)
```

time: 474 us -> 168 us (0.35)
  waiting for transfers between devices: 217 us -> 0 us
  Pallas kernels: 0 us -> 167 us
  local copies, waits for them, and re-layouts: 110 us -> 0 us
  other arithmetic: 60.8 us -> 0 us
  matrix products: 54.1 us -> 0 us
  starting transfers between devices: 29.3 us -> 0 us
    pallas_call x0 -> x2, Pallas kernels: none -> 167 us  [the longest x1 152 us: corner_turn(): pl.pallas_call(turn_kernel, out_shape=jax.ShapeDtypeStruct((4, 2, 32, GRO...]
    ppermute x4 -> x0, waiting for transfers between devices: 163 us -> none  [the longest x3 137 us: passed_along(): return lax.ppermute(value, axis, pairs)]
    dot_general x5 -> x0, matrix products: 54.1 us -> none  [the longest x4 28.7 us: correlate(): jnp.einsum('sirc,sjorc->ocij', turned, partner, preferred_element_type=jn...]
    all_to_all x1 -> x0, waiting for transfers between devices: 53.7 us -> none  [local(): lax.all_to_all(spectra, 'freq', split_axis=3, concat_axis=0, tiled=True)]
    while x11 -> x0, local copies, waits for them, and re-layouts: 43.2 us -> none  [the longest x2 23.9 us: local(): carried = lax.fori_loop(1, count, advance, (turned, visible))]
    neg x5 -> x0, other arithmetic: 25.8 us -> none  [the longest x1 16.5 us: dft_table(): upper = jnp.concatenate([cosine, -sine], axis=1)]
    reshape x2 -> x0, local copies, waits for them, and re-layouts: 23.5 us -> none  [local(): spectra.astype(jnp.bfloat16).reshape(frames, inputs_blk, 2, channels)]
    convert_element_type x2 -> x0, other arithmetic: 21.9 us -> none  [the longest x1 17.9 us: dft_table(): sine = (jnp.sin(phase) * factor).astype(jnp.bfloat16)]
  transfers between devices with their start and end apart: 5 -> 0, of which waited for: 5 -> 0; matrix products, arithmetic and copies ran while one was open for 8% -> 0% of each run, Pallas kernels for 0% -> 0%
where the time goes in v1:
time: 168 us; the launch traced here: 167 us
  Pallas kernels  167 us (99%)
    pallas_call x1, Pallas kernels, corner_turn(): pl.pallas_call(turn_kernel, out_shape=jax.ShapeDtypeStruct((4, 2, 32, GRO...  152 us
    pallas_call x1, Pallas kernels, correlate(): pl.pallas_call(functools.partial(correlate_kernel, count), grid=(GROUP //...  14.7 us

profile of v1, /device:TPU:1, one launch (start us, length us, event | category | flops | bytes accessed | tf_op | source)
XLA Modules:
  0.0 167.2 jit_solution(646097130397826656)
XLA Ops:
  0.0 152.5 %corner_turn.1 = bf16[4,2,32,32,8,128]{5,4,3,2,1,0:T(8,128)(2,1)} custom-call(s32[2,128,8192]{2,1,0:T(8,128)} %volts.1, s32[4,1024]{1,0:T(4,128)} %taps.1, bf16[1024,1024]{1,0:T(8,128)(2,1)} %constant.2.clone.table_hbm), custom_call_target="tpu_custom_call" | custom-call | tf_op jit(solution)/shard_map/corner_turn/pallas_call | solution.py:292
  152.5 14.7 %correlate.1 = f32[2,32,128,512]{3,2,1,0:T(8,128)} custom-call(bf16[4,64,32,8,128]{4,3,2,1,0:T(8,128)(2,1)} %bitcast.1), custom_call_target="tpu_custom_call" | custom-call | tf_op jit(solution)/shard_map/correlate/pallas_call | solution.py:344

commit v2 on v1

--- a/solution.py
+++ b/solution.py
@@ -18,6 +18,8 @@
 GROUP = 32
 PITCH = CHANNELS + 8
 CHUNK = 256
+FIRST = 7
+AHEAD = 4
 LAG = 8
 
 
@@ -45,12 +47,14 @@
 
 
 def offset(i):
-    return i % 4, (i // 4 + i) % 4
+    far = (i + 12) // 16
+    r = far * (i - 4)
+    return (1 - far) * i + far * (r // 3), far * (1 + r % 3)
 
 
 def turn_kernel(
     volts, taps, table_hbm, out,
-    frames, halo_out, halo_in, coeffs, weighted, table, spectra, outbox, inbox,
+    frames, lines, coeffs, weighted, table, spectra, outbox, inbox,
     load_sem, table_sem, halo_send, halo_recv, plane_send, plane_recv,
     y_send, y_recv, core_send, core_recv, dup_send, dup_recv, keep_sem,
 ):
@@ -65,6 +69,7 @@
     twin = device(x, y, z, 1 - c)
     after = ((f + 1) % 32, block)
     before = ((f + 31) % 32, block)
+    needs_us = ((f + 33 - 2 * c) % 32, block)
 
     def plane(i, sign):
         dx, dz = offset(i)
@@ -82,45 +87,51 @@
 
     lax.fori_loop(1, 16, greet, 0)
 
-    def load(s):
+    def load(p):
+        first = pl.multiple_of(((p + 5) % 8) * CHANNELS, CHANNELS)
         return pltpu.make_async_copy(
-            volts.at[:, :, pl.ds(s * CHANNELS, CHANNELS)], frames.at[s], load_sem.at[s]
+            volts.at[:, :, pl.ds(first, CHANNELS)], frames.at[p], load_sem.at[p]
         )
 
+    def fetch(t, carry):
+        load((3 * c + t) % 8).start()
+        return carry
+
     table_copy = pltpu.make_async_copy(table_hbm, table, table_sem)
-    for s in (5, 6, 7, 4, 3, 2, 1):
-        load(s).start()
+    lax.fori_loop(0, 8, fetch, 0)
     table_copy.start()
-    load(0).start()
 
     coeffs[...] = taps[...].astype(jnp.float32) * (1.0 / 1024.0)
 
-    for j in range(3):
-        load(5 + j).wait()
-
-        def narrow(t, carry):
-            rows = pl.ds(pl.multiple_of(t * 16, 16), 16)
+    def narrow(t, carry):
+        p = (3 * c + t) % 8
+        load(p).wait()
+
+        def body(i, carry):
+            rows = pl.ds(pl.multiple_of(i * 16, 16), 16)
             for r in range(2):
-                halo_out[j, r, rows, :] = frames[5 + j, r, rows, :].astype(jnp.bfloat16)
+                lines[0, p, r, rows, :] = frames[p, r, rows, :].astype(jnp.bfloat16)
             return carry
 
-        lax.fori_loop(0, INPUTS // 16, narrow, 0)
-
+        return lax.fori_loop(0, INPUTS // 16, body, carry)
+
+    lax.fori_loop(0, 4, narrow, 0)
     pl.semaphore_wait(barrier, 21)
+    theirs_first = pl.ds(3 * c, 4)
     halo = pltpu.make_async_remote_copy(
-        src_ref=halo_out, dst_ref=halo_in, send_sem=halo_send, recv_sem=halo_recv,
-        device_id=after, device_id_type=MESH,
+        src_ref=lines.at[0, theirs_first], dst_ref=lines.at[1, theirs_first], send_sem=halo_send,
+        recv_sem=halo_recv, device_id=needs_us, device_id_type=MESH,
     )
     halo.start()
-
-    def filter_half(earlier, first):
+    lax.fori_loop(4, 8, narrow, 0)
+
+    def filter_half(frame):
         def body(t, carry):
             rows = pl.ds(pl.multiple_of(t * 16, 16), 16)
             for r in range(2):
                 for n in range(0, CHANNELS, 256):
                     cols = slice(n, n + 256)
-                    seen = [earlier(j, r, rows, cols) for j in range(3)]
-                    seen += [frames[first + j, r, rows, cols].astype(jnp.float32) for j in range(4)]
+                    seen = [frame(j, r, rows, cols) for j in range(7)]
                     scale = [jnp.broadcast_to(coeffs[k : k + 1, cols], (16, 256)) for k in range(4)]
                     for s in range(4):
                         total = scale[0] * seen[s]
@@ -132,31 +143,37 @@
 
         lax.fori_loop(0, INPUTS // 16, body, 0)
 
-    def transform_half():
-        def body(s, carry):
-            rhs = weighted[s]
-            re = pl.multiple_of(s * PITCH, 8)
-            im = pl.multiple_of((4 + s) * PITCH, 8)
-            for q in range(HALF // CHUNK):
-                got = lax.dot_general(
-                    table[q * 2 * CHUNK : (q + 1) * 2 * CHUNK, :], rhs, (((1,), (1,)), ((), ())),
-                    preferred_element_type=jnp.float32,
-                )
-                a, b = got[:CHUNK, :INPUTS], got[CHUNK:, :INPUTS]
-                cc, d = got[:CHUNK, INPUTS:], got[CHUNK:, INPUTS:]
-                k = q * CHUNK
-                spectra[pl.ds(re + k, CHUNK), :] = a + d
-                spectra[pl.ds(im + k, CHUNK), :] = cc - b
-                spectra[pl.ds(re + HALF + k, CHUNK), :] = a - d
-                spectra[pl.ds(im + HALF + k, CHUNK), :] = cc + b
-                if q == 0:
-                    spectra[pl.ds(re, 1), :] = a[:1]
-                    spectra[pl.ds(im, 1), :] = cc[:1]
-                    spectra[pl.ds(re + CHANNELS, 1), :] = b[:1]
-                    spectra[pl.ds(im + CHANNELS, 1), :] = d[:1]
-            return carry
-
-        lax.fori_loop(0, 4, body, 0)
+    def late_frame(j, r, rows, cols):
+        return frames[(4 + j) % 8, r, rows, cols].astype(jnp.float32)
+
+    live = jnp.where((f + 31 * c) % 62 > 0, 1.0, 0.0).astype(jnp.float32)
+
+    def early_frame(j, r, rows, cols):
+        if j < 3:
+            return lines[1 - c, j, r, rows, cols].astype(jnp.float32) * live
+        return lines[c, j, r, rows, cols].astype(jnp.float32)
+
+    def transform(s):
+        rhs = weighted[s]
+        re = pl.multiple_of(s * PITCH, 8)
+        im = pl.multiple_of((4 + s) * PITCH, 8)
+        for q in range(HALF // CHUNK):
+            got = lax.dot_general(
+                table[q * 2 * CHUNK : (q + 1) * 2 * CHUNK, :], rhs, (((1,), (1,)), ((), ())),
+                preferred_element_type=jnp.float32,
+            )
+            a, b = got[:CHUNK, :INPUTS], got[CHUNK:, :INPUTS]
+            cc, d = got[:CHUNK, INPUTS:], got[CHUNK:, INPUTS:]
+            k = q * CHUNK
+            spectra[pl.ds(re + k, CHUNK), :] = a + d
+            spectra[pl.ds(im + k, CHUNK), :] = cc - b
+            spectra[pl.ds(re + HALF + k, CHUNK), :] = a - d
+            spectra[pl.ds(im + HALF + k, CHUNK), :] = cc + b
+            if q == 0:
+                spectra[pl.ds(re, 1), :] = a[:1]
+                spectra[pl.ds(im, 1), :] = cc[:1]
+                spectra[pl.ds(re + CHANNELS, 1), :] = b[:1]
+                spectra[pl.ds(im + CHANNELS, 1), :] = d[:1]
 
     def gather(g, into):
         for k in range(GROUP):
@@ -172,28 +189,24 @@
             recv_sem=plane_recv.at[h, here], device_id=to, device_id_type=MESH,
         )
 
-    def send_half(h):
-        def body(i, carry):
-            gather(plane(i, 1)[0], outbox.at[h, plane(i, 1)[0]])
-            plane_copy(h, i).start()
-            return carry
-
-        lax.fori_loop(1, 16, body, 0)
-        gather(here, inbox.at[h, here])
+    def collect(h, i):
+        g = plane(i, 1)[0]
+        gather(g, outbox.at[h, g])
 
     def forward(h, i):
         j = plane(i, -1)[0]
 
-        @pl.when(i > 0)
-        def _():
+        def arrive():
             pltpu.make_async_remote_copy(
                 src_ref=inbox.at[h, j], dst_ref=inbox.at[h, j], send_sem=plane_send.at[h],
                 recv_sem=plane_recv.at[h, j], device_id=twin, device_id_type=MESH,
             ).wait_recv()
 
+        pl.when(i > 0)(arrive)
+
         theirs = inbox.at[h, j, 1 - y_lo]
         ours = inbox.at[h, j, y_lo]
-        slot = out.at[block, h, y_lo * 16 + j]
+        slot = out.at[block, h, (y_lo * 16 + j + h * c) % 32]
         for way, (to, chunk) in enumerate(((up, theirs), (down, theirs), (across, ours))):
             pltpu.make_async_remote_copy(
                 src_ref=chunk, dst_ref=slot, send_sem=y_send.at[way], recv_sem=y_recv.at[way, h, j],
@@ -207,7 +220,7 @@
 
     def arrival(way, h, j):
         sender = (y + 3 - 2 * way) % 4 if way < 2 else (y + 2) % 4
-        return out.at[(sender // 2) * 2 + c, h, (sender % 2) * 16 + j]
+        return out.at[(sender // 2) * 2 + c, h, ((sender % 2) * 16 + j + h * c) % 32]
 
     def duplicate(h, i):
         j = plane(i, -1)[0]
@@ -222,51 +235,45 @@
                 device_id=twin, device_id_type=MESH,
             ).start()
 
-    for s in (4, 3, 2, 1):
-        load(s).wait()
-    filter_half(lambda j, r, rows, cols: frames[1 + j, r, rows, cols].astype(jnp.float32), 4)
+    def steps(first, stop, *bodies):
+        def run(i, carry):
+            for body in bodies:
+                body(i)
+            return carry
+
+        lax.fori_loop(first, stop, run, 0)
+
+    def step(k):
+        forward(k // 16, k % 16)
+
+        @pl.when(k >= LAG)
+        def _():
+            duplicate((k - LAG) // 16, (k - LAG) % 16)
+
+    def send(m):
+        plane_copy(m // 16, m % 16).start()
+
+    filter_half(late_frame)
     table_copy.wait()
-    transform_half()
-    send_half(0)
-
-    def first(i, carry):
-        forward(0, i)
-
-        @pl.when(i >= LAG)
-        def _():
-            duplicate(0, i - LAG)
-
-        return carry
-
-    lax.fori_loop(0, 16, first, 0)
-
-    load(0).wait()
-    halo.wait()
-    live = jnp.where(f > 0, 1.0, 0.0).astype(jnp.float32)
-    filter_half(lambda j, r, rows, cols: halo_in[j, r, rows, cols].astype(jnp.float32) * live, 0)
-    transform_half()
-    send_half(1)
-
-    def second(i, carry):
-        forward(1, i)
-
-        @pl.when(i < LAG)
-        def _():
-            duplicate(0, i + 16 - LAG)
-
-        @pl.when(i >= LAG)
-        def _():
-            duplicate(1, i - LAG)
-
-        return carry
-
-    lax.fori_loop(0, 16, second, 0)
-
-    def last(i, carry):
-        duplicate(1, i)
-        return carry
-
-    lax.fori_loop(16 - LAG, 16, last, 0)
+    steps(0, 4, transform)
+    gather(here, inbox.at[0, here])
+    step(0)
+    steps(1, FIRST, lambda i: collect(0, i), send)
+    steps(FIRST, 16, lambda i: collect(0, i))
+    steps(1, FIRST, step)
+    halo.wait_send()
+    steps(FIRST, FIRST + AHEAD, send)
+
+    halo.wait_recv()
+    filter_half(early_frame)
+    steps(0, 4, transform, lambda i: step(FIRST + i))
+    steps(FIRST + AHEAD, 16, send)
+    gather(here, inbox.at[1, here])
+    steps(1, 4, lambda i: collect(1, i), lambda i: send(16 + i))
+    steps(4, 16, lambda i: collect(1, i))
+    steps(FIRST + 4, FIRST + 16, step, lambda k: send(k + 16 - FIRST))
+    steps(FIRST + 16, 32, step)
+    steps(32 - LAG, 32, lambda k: duplicate(k // 16, k % 16))
 
     def whole(ref, send_sem, recv_sem):
         return pltpu.make_async_remote_copy(
@@ -300,8 +307,7 @@
         out_specs=pl.BlockSpec(memory_space=pl.ANY),
         scratch_shapes=[
             pltpu.VMEM((FRAMES, 2, INPUTS, CHANNELS), jnp.int32),
-            pltpu.VMEM((3, 2, INPUTS, CHANNELS), bf16),
-            pltpu.VMEM((3, 2, INPUTS, CHANNELS), bf16),
+            pltpu.VMEM((2, 8, 2, INPUTS, CHANNELS), bf16),
             pltpu.VMEM((4, CHANNELS), jnp.float32),
             pltpu.VMEM((4, 2 * INPUTS, CHANNELS), bf16),
             pltpu.VMEM((CHANNELS, CHANNELS), bf16),

time: 168 us -> 144 us (0.86)
  Pallas kernels: 167 us -> 144 us
    pallas_call x1, Pallas kernels: 152 us -> 129 us  [corner_turn(): pl.pallas_call(turn_kernel, out_shape=jax.ShapeDtypeStruct((4, 2, 32, GRO...]
where the time goes in v2:
time: 144 us
  Pallas kernels  144 us (100%)
    pallas_call x1, Pallas kernels, corner_turn(): pl.pallas_call(turn_kernel, out_shape=jax.ShapeDtypeStruct((4, 2, 32, GRO...  129 us
    pallas_call x1, Pallas kernels, correlate(): pl.pallas_call(functools.partial(correlate_kernel, count), grid=(GROUP //...  14.7 us

profile of v2, /device:TPU:1, one launch (start us, length us, event | category | flops | bytes accessed | tf_op | source)
XLA Modules:
  0.0 143.5 jit_solution(12632217828616778214)
XLA Ops:
  0.0 128.8 %corner_turn.1 = bf16[4,2,32,32,8,128]{5,4,3,2,1,0:T(8,128)(2,1)} custom-call(s32[2,128,8192]{2,1,0:T(8,128)} %volts.1, s32[4,1024]{1,0:T(4,128)} %taps.1, bf16[1024,1024]{1,0:T(8,128)(2,1)} %constant.2.clone.table_hbm), custom_call_target="tpu_custom_call" | custom-call | tf_op jit(solution)/shard_map/corner_turn/pallas_call | solution.py:299
  128.8 14.7 %correlate.1 = f32[2,32,128,512]{3,2,1,0:T(8,128)} custom-call(bf16[4,64,32,8,128]{4,3,2,1,0:T(8,128)(2,1)} %bitcast.1), custom_call_target="tpu_custom_call" | custom-call | tf_op jit(solution)/shard_map/correlate/pallas_call | solution.py:350

commit v3 on v2

--- a/solution.py
+++ b/solution.py
@@ -298,13 +298,13 @@
     dma = pltpu.SemaphoreType.DMA
     return pl.pallas_call(
         turn_kernel,
-        out_shape=jax.ShapeDtypeStruct((4, 2, 32, GROUP, 8, INPUTS), bf16),
+        out_shape=pltpu.VMEM((4, 2, 32, GROUP, 8, INPUTS), bf16),
         in_specs=[
             pl.BlockSpec(memory_space=pl.ANY),
             pl.BlockSpec(memory_space=pltpu.VMEM),
             pl.BlockSpec(memory_space=pl.ANY),
         ],
-        out_specs=pl.BlockSpec(memory_space=pl.ANY),
+        out_specs=pl.BlockSpec(memory_space=pltpu.VMEM),
         scratch_shapes=[
             pltpu.VMEM((FRAMES, 2, INPUTS, CHANNELS), jnp.int32),
             pltpu.VMEM((2, 8, 2, INPUTS, CHANNELS), bf16),
@@ -318,7 +318,7 @@
             dma((3,)), dma((3, 2, 16)), dma, dma, dma((3,)), dma((3,)), dma,
         ],
         compiler_params=pltpu.CompilerParams(
-            collective_id=0, has_side_effects=True, vmem_limit_bytes=56 << 20
+            collective_id=0, has_side_effects=True, vmem_limit_bytes=40 << 20
         ),
         name="corner_turn",
     )(voltages, taps, table)
@@ -326,18 +326,19 @@
 
 def correlate_kernel(count, tiles, visible):
     me = lax.axis_index("blk")
+    base = pl.program_id(0) * count
     part = lax.broadcasted_iota(jnp.int32, (1, 8, INPUTS), 1)
     sign = jnp.where(part < 4, 0.0625, -0.0625).astype(jnp.float32)
     rows = 64 * 8
     for k in range(count):
-        mine = tiles[me, :, k].astype(jnp.float32)
+        mine = tiles[me, :, :, base + k].astype(jnp.float32).reshape(64, 8, INPUTS)
         rotated = pltpu.roll(mine, 4, axis=1) * sign
         left = jnp.concatenate(
             [(mine * 0.0625).reshape(rows, INPUTS), rotated.reshape(rows, INPUTS)], axis=1
         ).astype(jnp.bfloat16)
         for b in range(0, 4, 2):
             right = jnp.concatenate(
-                [tiles[b, :, k].reshape(rows, INPUTS), tiles[b + 1, :, k].reshape(rows, INPUTS)], axis=1
+                [tiles[b, :, :, base + k].reshape(rows, INPUTS), tiles[b + 1, :, :, base + k].reshape(rows, INPUTS)], axis=1
             )
             both = lax.dot_general(
                 left, right, (((0,), (0,)), ((), ())), preferred_element_type=jnp.float32
@@ -350,7 +351,7 @@
     return pl.pallas_call(
         functools.partial(correlate_kernel, count),
         grid=(GROUP // count,),
-        in_specs=[pl.BlockSpec((4, 64, count, 8, INPUTS), lambda k: (0, 0, k, 0, 0))],
+        in_specs=[pl.BlockSpec(memory_space=pltpu.VMEM)],
         out_specs=pl.BlockSpec((2, count, INPUTS, 4 * INPUTS), lambda k: (0, k, 0, 0)),
         out_shape=jax.ShapeDtypeStruct((2, GROUP, INPUTS, 4 * INPUTS), jnp.float32),
         compiler_params=pltpu.CompilerParams(vmem_limit_bytes=40 << 20),
@@ -361,7 +362,7 @@
 def local(voltages, taps):
     table = jnp.asarray(fourier_rows())
     tiles = corner_turn(voltages, taps, table)
-    return correlate(tiles.reshape(4, 64, GROUP, 8, INPUTS))
+    return correlate(pltpu.with_memory_space_constraint(tiles, pltpu.VMEM))
 
 
 def solution(mesh):

time: 144 us -> 138 us (0.958)
  Pallas kernels: 144 us -> 138 us
    pallas_call x1, Pallas kernels: 14.7 us -> 9.38 us  [correlate(): pl.pallas_call(functools.partial(correlate_kernel, count), grid=(GROUP //...]
where the time goes in v3:
time: 138 us
  Pallas kernels  138 us (100%)
    pallas_call x1, Pallas kernels, corner_turn(): pl.pallas_call(turn_kernel, out_shape=pltpu.VMEM((4, 2, 32, GROUP, 8, INP...  128 us
    pallas_call x1, Pallas kernels, correlate(): pl.pallas_call(functools.partial(correlate_kernel, count), grid=(GROUP //...  9.38 us

profile of v3, /device:TPU:1, one launch (start us, length us, event | category | flops | bytes accessed | tf_op | source)
XLA Modules:
  0.0 137.7 jit_solution(13378941671011459078)
XLA Ops:
  0.0 128.3 %corner_turn.1.tiles = bf16[4,2,32,32,8,128]{5,4,3,2,1,0:T(8,128)(2,1)S(1)} custom-call(s32[2,128,8192]{2,1,0:T(8,128)} %volts.1, s32[4,1024]{1,0:T(4,128)} %taps.1, bf16[1024,1024]{1,0:T(8,128)(2,1)} %constant.2.clone.table_hbm), custom_call_target="tpu_custom_call" | custom-call | tf_op jit(solution)/shard_map/corner_turn/pallas_call | solution.py:299
  128.3 9.4 %correlate.1 = f32[2,32,128,512]{3,2,1,0:T(8,128)} custom-call(bf16[4,2,32,32,8,128]{5,4,3,2,1,0:T(8,128)(2,1)S(1)} %corner_turn.1.tiles), custom_call_target="tpu_custom_call" | custom-call | tf_op jit(solution)/shard_map/correlate/pallas_call | solution.py:351

commit v4 on v3

--- a/solution.py
+++ b/solution.py
@@ -49,7 +49,7 @@
 def offset(i):
     far = (i + 12) // 16
     r = far * (i - 4)
-    return (1 - far) * i + far * (r // 3), far * (1 + r % 3)
+    return (1 - far) * i + far * (r // 3), far * (1 + (r + 1) % 3)
 
 
 def turn_kernel(

time: 138 us -> 137 us (level); the launches traced: 138 us -> 135 us
  Pallas kernels: 138 us -> 135 us
    pallas_call x1, Pallas kernels: 128 us -> 126 us  [corner_turn(): pl.pallas_call(turn_kernel, out_shape=pltpu.VMEM((4, 2, 32, GROUP, 8, INP...]
where the time goes in v4:
time: 137 us; the launch traced here: 135 us
  Pallas kernels  135 us (99%)
    pallas_call x1, Pallas kernels, corner_turn(): pl.pallas_call(turn_kernel, out_shape=pltpu.VMEM((4, 2, 32, GROUP, 8, INP...  126 us
    pallas_call x1, Pallas kernels, correlate(): pl.pallas_call(functools.partial(correlate_kernel, count), grid=(GROUP //...  9.38 us

profile of v4, /device:TPU:1, one launch (start us, length us, event | category | flops | bytes accessed | tf_op | source)
XLA Modules:
  0.0 135.2 jit_solution(2032933561705203750)
XLA Ops:
  0.0 125.8 %corner_turn.1.tiles = bf16[4,2,32,32,8,128]{5,4,3,2,1,0:T(8,128)(2,1)S(1)} custom-call(s32[2,128,8192]{2,1,0:T(8,128)} %volts.1, s32[4,1024]{1,0:T(4,128)} %taps.1, bf16[1024,1024]{1,0:T(8,128)(2,1)} %constant.2.clone.table_hbm), custom_call_target="tpu_custom_call" | custom-call | tf_op jit(solution)/shard_map/corner_turn/pallas_call | solution.py:299
  125.8 9.4 %correlate.1 = f32[2,32,128,512]{3,2,1,0:T(8,128)} custom-call(bf16[4,2,32,32,8,128]{5,4,3,2,1,0:T(8,128)(2,1)S(1)} %corner_turn.1.tiles), custom_call_target="tpu_custom_call" | custom-call | tf_op jit(solution)/shard_map/correlate/pallas_call | solution.py:351
